TPU v7x, 32 devices: a whole 2x2x4 slice. The times are simulated.
32 devices in a mesh: group: 2 (over y), seq: 4 (over z), shard: 2 (over x), guide: 2 (over core).
Axes of the slice: x: 2, y: 2, z: 4, core: 2. Of those that a mesh axis runs over, the one named last changes fastest.
Arguments:
- queries: bfloat16 [2, 2, 512, 2560], P('guide', 'group', 'seq', 'shard'), parts along dimension 1, may hold values from -120 to 120
- key_vecs: bfloat16 [2, 2, 512, 2560], P('guide', 'group', 'seq', 'shard'), parts along dimension 1, may hold values from -4 to 4
- value_vecs: bfloat16 [2, 2, 512, 2560], P('guide', 'group', 'seq', 'shard'), parts along dimension 1, may hold values from -24 to 24
- residual: bfloat16 [2, 2, 512, 5120], P('guide', 'group', 'seq', 'shard'), parts along dimension 1, may hold values from -64 to 64
- w_out: bfloat16 [2560, 5120], P('shard', 'guide'), may hold values from -0.125 to 0.125
- attn_gate: float32 [2, 5120], P('group', 'shard'), parts along dimension 0, may hold values from 2 to 4
- norm_shift: float32 [2, 5120], P('group', 'shard'), parts along dimension 0, may hold values from -3 to 3
- norm_scale: float32 [2, 5120], P('group', 'shard'), parts along dimension 0, may hold values from -2.5 to 2.5
- w_head: bfloat16 [5120, 64], P('shard'), may hold values from -0.078125 to 0.078125
- noise: float32 [2, 4, 128, 64], P('group', 'seq', None, 'guide'), parts along dimension 0, may hold values from -6 to 6
- timesteps: int32 [2], P('group'), parts along dimension 0, may hold values from 100 to 980
- frame_owner: int32 [2, 4], P('group'), parts along dimension 0, may hold values from 0 to 3, each once within a row
Outputs:
- sds_grad: float32 [2, 4, 128, 64], P('group', 'seq', None, 'guide'), parts along dimension 0
There are 2 independent parts, one for each index of `group`. A program takes and returns all parts, laid end to end along the dimension named above; an argument that names none is the same for every part. Nothing has to cross between parts.
Inputs may be any that keep to these rules, and one draw needn't show every extreme that they name: `frame_owner`: each row names every owner index once.
All inputs are finite; a program needn't handle non-finite values.
Results may differ from a plain program's by a relative error of at most 0.003.
Values may be sent and summed in bfloat16 or wider, within the bound.
No kernel may reach another device: no remote copies, remote signals or barrier semaphores. Data moves between devices by JAX's collectives and lax.ppermute only.
A program may use at most 128 MiB of HBM per device.

v0:
```python
import jax
import jax.numpy as jnp
from jax import lax
from jax.sharding import PartitionSpec as P

D = 5120
HEAD_DIM = 128


beta_low = 0.0001
beta_high = 0.02
guidance_scale = 3.0
norm_epsilon = 1e-06


def plan_weight(timesteps):
    steps_float = timesteps.astype(jnp.float32)
    exponent = (steps_float + 1.0) * beta_low + (beta_high - beta_low) * steps_float * (
        steps_float + 1.0
    ) / (2.0 * 999.0)
    return 1.0 - jnp.exp(-exponent)


def softmax_absorb(query_block, carry_state, pieces):
    running_top, running_total, running_acc = carry_state
    keys_block, values_block = pieces
    heads_local = query_block.shape[2]
    keys_split = keys_block.reshape(keys_block.shape[0], keys_block.shape[1], heads_local, HEAD_DIM)
    values_split = values_block.reshape(
        values_block.shape[0], values_block.shape[1], heads_local, HEAD_DIM
    )
    scores = jnp.einsum(
        "tqhd,tkhd->tqhk", query_block, keys_split, preferred_element_type=jnp.float32
    ) * HEAD_DIM ** (-0.5)
    new_top = jnp.max(scores, axis=-1)
    factor = jnp.exp(running_top - new_top)
    expo = jnp.exp(scores - new_top[..., None])
    new_total = running_total * factor + jnp.sum(expo, axis=-1)
    update = jnp.einsum(
        "tqhk,tkhd->tqhd",
        expo.astype(jnp.bfloat16),
        values_split,
        preferred_element_type=jnp.float32,
    )
    return (new_top, new_total, running_acc * factor[..., None] + update)


def start_state(step_count, token_count, heads_local):
    return (
        jnp.full((step_count, token_count, heads_local), -jnp.inf, jnp.float32),
        jnp.zeros((step_count, token_count, heads_local), jnp.float32),
        jnp.zeros((step_count, token_count, heads_local, HEAD_DIM), jnp.float32),
    )


def on_device(
    queries,
    key_vecs,
    value_vecs,
    residual,
    w_out,
    attn_gate,
    norm_shift,
    norm_scale,
    w_head,
    noise,
    timesteps,
    frame_owner,
):
    query_local = queries[0]
    step_count, token_count, width_local = query_local.shape
    heads_local = width_local // HEAD_DIM
    query_split = query_local.reshape(step_count, token_count, heads_local, HEAD_DIM)
    final_state = softmax_absorb(
        query_split,
        start_state(step_count, token_count, heads_local),
        (
            lax.all_gather(key_vecs[0], "seq", axis=1, tiled=True),
            lax.all_gather(value_vecs[0], "seq", axis=1, tiled=True),
        ),
    )
    total_sum = final_state[1]
    acc_sum = final_state[2]
    row_count = step_count * token_count
    attended = (acc_sum / total_sum[..., None]).astype(jnp.bfloat16).reshape(row_count, width_local)
    both_rows = jnp.dot(
        lax.all_gather(attended, "guide", axis=0, tiled=True),
        w_out,
        preferred_element_type=jnp.float32,
    )
    half_width = w_out.shape[1]
    swapped = lax.all_to_all(
        both_rows.reshape(2, row_count, half_width),
        "guide",
        split_axis=0,
        concat_axis=2,
        tiled=True,
    )
    projected = swapped.reshape(row_count, 2 * half_width)
    attn_out = lax.psum_scatter(projected, "shard", scatter_dimension=1, tiled=True)
    width_shard = attn_out.shape[1]
    hidden = residual[0].astype(jnp.float32) + attn_gate[:, None, :] * attn_out.reshape(
        step_count, token_count, width_shard
    )
    sum_first = jnp.sum(hidden, axis=-1)
    sum_second = jnp.sum(hidden * hidden, axis=-1)
    sum_first, sum_second = lax.psum((sum_first, sum_second), "shard")
    mean_row = sum_first / D
    var_row = sum_second / D - mean_row * mean_row
    inv_std = lax.rsqrt(var_row + norm_epsilon)
    modulated = (hidden - mean_row[..., None]) * inv_std[..., None] * (
        1.0 + norm_scale[:, None, :]
    ) + norm_shift[:, None, :]
    head_float = w_head.astype(jnp.float32)
    partial_head = jnp.einsum("tqd,dc->tqc", modulated, head_float, precision=lax.Precision.HIGHEST)
    predicted = lax.psum(partial_head, "shard")
    seq_count = lax.axis_size("seq")
    frame_group = token_count // seq_count
    channels = predicted.shape[-1]
    frames_view = predicted.reshape(step_count, seq_count, frame_group, channels)
    owner_table = (
        frame_owner[:, :, None] == jnp.arange(seq_count, dtype=jnp.int32)[None, None, :]
    ).astype(jnp.float32)
    by_owner = jnp.einsum(
        "tfo,tfgc->togc", owner_table, frames_view, precision=lax.Precision.HIGHEST
    )
    weight = plan_weight(timesteps)
    arrived = lax.all_to_all(
        lax.all_to_all(by_owner[None], "seq", split_axis=2, concat_axis=3, tiled=True),
        "guide",
        split_axis=4,
        concat_axis=0,
        tiled=True,
    )
    guided = arrived[1] + guidance_scale * (arrived[0] - arrived[1])
    return weight[:, None, None, None] * (guided - noise)


def solution(mesh):
    return jax.shard_map(
        on_device,
        mesh=mesh,
        in_specs=(
            P("guide", "group", "seq", "shard"),
            P("guide", "group", "seq", "shard"),
            P("guide", "group", "seq", "shard"),
            P("guide", "group", "seq", "shard"),
            P("shard", "guide"),
            P("group", "shard"),
            P("group", "shard"),
            P("group", "shard"),
            P("shard", None),
            P("group", "seq", None, "guide"),
            P("group"),
            P("group", None),
        ),
        out_specs=P("group", "seq", None, "guide"),
        check_vma=False,
    )
```

profile of v0, /device:TPU:0, one launch (start us, length us, event | category | flops | bytes accessed | tf_op | source)
XLA Modules:
  0.0 175.5 jit_solution(11851235863250960437)
XLA Ops:
  6.5 1.9 %copy.44 = bf16[1,1,128,1280]{2,3,1,0:T(8,128)(2,1)} copy(bf16[1,1,128,1280]{3,2,1,0:T(8,128)(2,1)} %param.13) | data formatting | bytes 655360 | tf_op args[1]
  8.5 0.7 all-gather.7.cloned.1.call-update
  9.5 35.6 %all-gather.5.cloned.1.call-done = bf16[1,1,512,1280]{2,3,1,0:T(8,128)(2,1)} async-done(((bf16[1,1,128,1280]{2,3,1,0:T(8,128)(2,1)}), bf16[1,1,512,1280]{2,3,1,0:T(8,128)(2,1)}) %all-gather.5.cloned.1.call-update) | async-done | bytes 1310736 | tf_op jit(solution)/shard_map/all_gather | solution.py:78
  45.1 1.9 %bitcast_reduce_fusion = (f32[128,10]{0,1:T(8,128)S(1)}, f32[10,512,128]{2,1,0:T(8,128)S(1)}) fusion(bf16[512,10,128]{0,2,1:T(8,128)(2,1)} %bitcast.120, bf16[128,10,128]{0,2,1:T(8,128)(2,1)S(1)} %bitcast.119), kind=kOutput, calls=%fused_computation.1 | convolution fusion | flops 169081600 | bytes 4264960 | tf_op jit(solution)/shard_map/tqhd,tkhd->tqhk/dot_general | solution.py:32
  47.5 30.0 %all-gather.7.cloned.1.call-done = bf16[1,1,512,1280]{3,2,1,0:T(8,128)(2,1)} async-done(((bf16[1,1,128,1280]{3,2,1,0:T(8,128)(2,1)}), bf16[1,1,512,1280]{3,2,1,0:T(8,128)(2,1)}) %all-gather.7.cloned.1.call-update) | async-done | bytes 1310736 | tf_op jit(solution)/shard_map/all_gather | solution.py:79
  77.5 2.4 %copy.48 = bf16[1,1,512,1280]{2,3,1,0:T(8,128)(2,1)} copy(bf16[1,1,512,1280]{3,2,1,0:T(8,128)(2,1)} %all-gather.7.cloned.1.call-done) | data formatting | bytes 2621440 | tf_op jit(solution)/shard_map/all_gather | solution.py:79
  79.9 2.1 %fusion.22 = bf16[1,128,10,128]{1,3,2,0:T(8,128)(2,1)S(1)} fusion(bf16[512,10,128]{0,2,1:T(8,128)(2,1)} %bitcast.121, f32[10,512,128]{2,1,0:T(8,128)S(1)} %get-tuple-element.14, f32[128,10]{0,1:T(8,128)S(1)} %get-tuple-element.13, f32[128,10]{0,1:T(8,128)S(1)} %get-tuple-element.10, f32[128,10]{0,1:T(8,128)S(1)} %get-tuple-element.9), kind=kOutput, calls=%fused_computation.19 | convolution fusion | flops 170229760 | bytes 4275200 | tf_op jit(solution)/shard_map/tqhk,tkhd->tqhd/dot_general | solution.py:39
  82.0 2.3 %all_gather.11 = bf16[256,1280]{0,1:T(8,128)(2,1)S(1)} all-gather(bf16[128,1280]{0,1:T(8,128)(2,1)S(1)} %bitcast.122), channel_id=1, replica_groups=mesh['group'=2,'seq'=4,'shard'=2,'guide'=2] {'guide'}, dimensions={0}, use_global_device_ids=true | all-gather | bytes 983040 | tf_op jit(solution)/shard_map/all_gather | solution.py:87
  84.3 4.7 %fusion.40 = f32[256,2560]{1,0:T(8,128)S(1)} fusion(bf16[256,1280]{0,1:T(8,128)(2,1)S(1)} %all_gather.11, bf16[1280,2560]{1,0:T(8,128)(2,1)} %param.16), kind=kOutput, calls=%fused_computation.43 | convolution fusion | flops 1677721600 | bytes 9830400 | tf_op jit(solution)/shard_map/dot_general | solution.py:86
  89.1 5.8 %all_to_all.42 = f32[2,128,2560]{2,1,0:T(8,128)S(1)} all-to-all(f32[2,128,2560]{2,1,0:T(8,128)S(1)} %bitcast.115), channel_id=1, replica_groups=mesh['group'=2,'seq'=4,'shard'=2,'guide'=2] {'guide'}, dimensions={0} | all-to-all | bytes 5242880 | tf_op jit(solution)/shard_map/all_to_all | solution.py:92
  94.9 2.0 %copy.50 = f32[1,128,2,2560]{3,2,1,0:T(2,128)S(1)} copy(f32[1,128,2,2560]{3,1,2,0:T(8,128)S(1)} %bitcast.117) | data formatting | bytes 5242880 | tf_op jit(solution)/shard_map/all_to_all | solution.py:92
  96.9 2.0 %copy.63 = f32[16,8,2,2560]{3,1,2,0:T(8,128)} copy(f32[16,8,2,2560]{3,2,1,0:T(2,128)S(1)} %bitcast.118) | data formatting | bytes 5242880
  98.9 0.7 copy-done.5
  99.7 36.1 %reduce-scatter.2.cloned.1.call-done = f32[128,2560]{1,0:T(8,128)} async-done(((f32[128,5120]{1,0:T(8,128)}), f32[128,2560]{1,0:T(8,128)}) %reduce-scatter.2.cloned.1.call-update) | async-done | bytes 1310736 | tf_op jit(solution)/shard_map/reduce_scatter | solution.py:100
  135.9 1.8 %fusion.29 = (f32[128]{0:T(128)S(1)}, f32[128]{0:T(128)S(1)}) fusion(f32[128,2560]{1,0:T(8,128)} %reduce-scatter.2.cloned.1.call-done, f32[2560]{0:T(1024)S(1)} %reduce.6, bf16[1,1,128,2560]{3,2,1,0:T(8,128)(2,1)S(1)} %copy-done.2), kind=kLoop, calls=%fused_computation.25 | loop fusion | flops 1965824 | bytes 1977344 | tf_op jit(solution)/shard_map/reduce_sum | solution.py:105
  137.6 4.9 %all-reduce = (f32[1,128]{1,0:T(1,128)S(1)}, f32[1,128]{1,0:T(1,128)S(1)}) all-reduce(f32[1,128]{1,0:T(1,128)S(1)} %bitcast.130, f32[1,128]{1,0:T(1,128)S(1)} %bitcast.129), channel_id=1, replica_groups=mesh['group'=2,'seq'=4,'shard'=2,'guide'=2] {'shard'}, use_global_device_ids=true, to_apply=%region_6.0 | all-reduce | flops 256 | bytes 2048 | tf_op jit(solution)/shard_map/psum | solution.py:107
  142.6 1.0 fusion.6
  143.7 7.8 %psum.23 = f32[4,32,64]{2,0,1:T(4,128)S(1)} all-reduce(f32[4,32,64]{2,0,1:T(4,128)S(1)} %copy.52), channel_id=1, replica_groups=mesh['group'=2,'seq'=4,'shard'=2,'guide'=2] {'shard'}, use_global_device_ids=true, to_apply=%region_7.0 | all-reduce | flops 8192 | bytes 65536 | tf_op jit(solution)/shard_map/psum | solution.py:116
  151.8 0.7 reshape.232
  152.5 5.0 %all-to-all-start.1 = ((f32[4,1,2048]{2,1,0:T(1,128)}), f32[4,1,2048]{2,1,0:T(1,128)S(1)}, u32[]{:S(2)}, u32[]{:S(2)}) async-start(f32[4,1,2048]{2,1,0:T(1,128)} %reshape.232), calls=%async_computation.2 | async-start | bytes 65536 | tf_op jit(solution)/shard_map/all_to_all | solution.py:129
  158.2 5.0 %all-to-all-done.1 = f32[4,1,2048]{2,1,0:T(1,128)S(1)} async-done(((f32[4,1,2048]{2,1,0:T(1,128)}), f32[4,1,2048]{2,1,0:T(1,128)S(1)}, u32[]{:S(2)}, u32[]{:S(2)}) %all-to-all-start.1) | async-done | bytes 32800 | tf_op jit(solution)/shard_map/all_to_all | solution.py:129
  163.7 0.7 reduce.10
  164.6 3.8 %all_to_all.43 = f32[1,1,1,128,64]{3,2,1,0,4:T(1,128)S(1)} all-to-all(f32[1,1,1,128,64]{3,2,1,0,4:T(1,128)S(1)} %copy.55), channel_id=1, replica_groups=mesh['group'=2,'seq'=4,'shard'=2,'guide'=2] {'guide'}, dimensions={4} | all-to-all | bytes 65536 | tf_op jit(solution)/shard_map/all_to_all | solution.py:128
  168.4 0.6 fusion.34
  (35 shorter events, 2.0 us)
Async XLA Ops:
  6.5 136.0 %copy-start = (bf16[2560,64]{0,1:T(8,128)(2,1)S(1)}, bf16[2560,64]{0,1:T(8,128)(2,1)}, u32[]{:S(2)}) copy-start(bf16[2560,64]{0,1:T(8,128)(2,1)} %param.20) | copy-start | bytes 983044
  6.5 2.8 %copy-start.3 = (bf16[1,1,128,1280]{3,2,1,0:T(8,128)(2,1)S(1)}, bf16[1,1,128,1280]{3,2,1,0:T(8,128)(2,1)}, u32[]{:S(2)}) copy-start(bf16[1,1,128,1280]{3,2,1,0:T(8,128)(2,1)} %param.12) | copy-start | bytes 983044
  6.5 38.6 %all-gather.5.cloned.1.call-start = ((), (), s32[]{:S(2)}) async-start(), calls=%async_computation.5 | async-start | bytes 1638400 | tf_op jit(solution)/shard_map/all_gather | solution.py:78
  8.5 69.0 %all-gather.7.cloned.1.call-start = ((), (), s32[]{:S(2)}) async-start(), calls=%async_computation.6 | async-start | bytes 1638400 | tf_op jit(solution)/shard_map/all_gather | solution.py:79
  9.2 126.6 %reduce-scatter.2.cloned.1.call-start = ((), (), s32[]{:S(2)}) async-start(), calls=%async_computation.4 | async-start | bytes 3932160 | tf_op jit(solution)/shard_map/reduce_scatter | solution.py:100
  98.9 0.7 copy-start.5
  98.9 0.7 copy-start.6
  98.9 0.8 copy-start.7
  98.9 37.0 %copy-start.2 = (bf16[1,1,128,2560]{3,2,1,0:T(8,128)(2,1)S(1)}, bf16[1,1,128,2560]{3,2,1,0:T(8,128)(2,1)}, u32[]{:S(2)}) copy-start(bf16[1,1,128,2560]{3,2,1,0:T(8,128)(2,1)} %param.15) | copy-start | bytes 1966084
  135.9 6.7 %copy-start.1 = (f32[128,2560]{1,0:T(8,128)S(1)}, f32[128,2560]{1,0:T(8,128)}, u32[]{:S(2)}) copy-start(f32[128,2560]{1,0:T(8,128)} %reduce-scatter.2.cloned.1.call-done) | copy-start | bytes 3932164
  142.6 8.9 %copy-start.8 = (s32[1,4]{1,0:T(1,128)S(1)}, s32[1,4]{1,0:T(1,128)}, u32[]{:S(2)}) copy-start(s32[1,4]{1,0:T(1,128)} %param.23) | copy-start | bytes 52
  142.6 25.8 %copy-start.4 = (f32[1,1,128,32]{2,3,1,0:T(8,128)S(1)}, f32[1,1,128,32]{2,3,1,0:T(8,128)}, u32[]{:S(2)}) copy-start(f32[1,1,128,32]{2,3,1,0:T(8,128)} %param.21) | copy-start | bytes 49156
  152.5 10.7 %all-to-all-start.1 = ((f32[4,1,2048]{2,1,0:T(1,128)}), f32[4,1,2048]{2,1,0:T(1,128)S(1)}, u32[]{:S(2)}, u32[]{:S(2)}) async-start(f32[4,1,2048]{2,1,0:T(1,128)} %reshape.232), calls=%async_computation.2 | async-start | bytes 65536 | tf_op jit(solution)/shard_map/all_to_all | solution.py:129
Sparse Core Ops, SparseCore 0:
  8.9 36.1 all-gather.4
  46.7 30.7 all-gather.6
  99.0 36.7 reduce-scatter.1
where the time goes:
time: 176 us
  waiting for transfers between devices  107 us (61%)
  blocking collectives  24.6 us (14%)
  between operations  14 us (8%)
  local copies, waits for them, and re-layouts  10.7 us (6%)
  matrix products  10.1 us (6%)
  starting transfers between devices  5.09 us (3%)
  other arithmetic  3.65 us (2%)
    reduce_scatter x1, waiting for transfers between devices, on_device(): lax.psum_scatter(projected, 'shard', scatter_dimension=1, tiled=True)  36.1 us
    all_gather x1, waiting for transfers between devices, on_device(): lax.all_gather(key_vecs[0], 'seq', axis=1, tiled=True)  35.6 us
    all_gather x1, waiting for transfers between devices, on_device(): lax.all_gather(value_vecs[0], 'seq', axis=1, tiled=True)  30 us
    psum x1, blocking collectives, on_device(): predicted = lax.psum(partial_head, 'shard')  7.79 us
    all_to_all x1, blocking collectives, on_device(): lax.all_to_all(both_rows.reshape(2, row_count, half_width), 'guide', spli...  5.84 us
    unnamed x23, local copies, waits for them, and re-layouts  5.6 us
    all_to_all x1, starting transfers between devices, on_device(): lax.all_to_all(by_owner[None], 'seq', split_axis=2, concat_axis=3, tiled=...  5.01 us
    all_to_all x1, waiting for transfers between devices, on_device(): lax.all_to_all(by_owner[None], 'seq', split_axis=2, concat_axis=3, tiled=...  4.96 us
  transfers between devices with their start and end apart: 4, of which 4 were waited for; matrix products, arithmetic and copies ran while one was open for 2% of the time, Pallas kernels for 0%

commit v1 on v0

v1 whole, which is shorter than its diff:
```python
import functools

import jax
import jax.numpy as jnp
from jax import lax
from jax.experimental import pallas as pl
from jax.experimental.pallas import tpu as pltpu
from jax.sharding import PartitionSpec as P

HEAD_DIM = 128
LANES = 128
SUBLANES = 8
beta_low = 0.0001
beta_high = 0.02
guidance_scale = 3.0
norm_epsilon = 1e-06
LOG2E = 1.4426950408889634

F32 = jnp.float32
BF16 = jnp.bfloat16
VMEM_SPEC = pl.BlockSpec(memory_space=pltpu.VMEM)
SMEM_SPEC = pl.BlockSpec(memory_space=pltpu.SMEM)
ANY_SPEC = pl.BlockSpec(memory_space=pl.ANY)


def plan_weight(timesteps):
    steps_float = timesteps.astype(jnp.float32)
    exponent = (steps_float + 1.0) * beta_low + (beta_high - beta_low) * steps_float * (
        steps_float + 1.0
    ) / (2.0 * 999.0)
    return 1.0 - jnp.exp(-exponent)


def attend_all(query_split, keys_all, values_all):
    heads_local = query_split.shape[2]
    keys_split = keys_all.reshape(keys_all.shape[0], keys_all.shape[1], heads_local, HEAD_DIM)
    values_split = values_all.reshape(values_all.shape[0], values_all.shape[1], heads_local, HEAD_DIM)
    scores = jnp.einsum(
        "tqhd,tkhd->tqhk", query_split, keys_split, preferred_element_type=F32
    ) * HEAD_DIM ** (-0.5)
    expo = jnp.exp(scores - jnp.max(scores, axis=-1, keepdims=True))
    total = jnp.sum(expo, axis=-1)
    mixed = jnp.einsum("tqhk,tkhd->tqhd", expo.astype(BF16), values_split, preferred_element_type=F32)
    return (mixed / total[..., None]).astype(BF16)


def general_plan(
    queries, key_vecs, value_vecs, residual, w_out, attn_gate, norm_shift, norm_scale, w_head, noise,
    timesteps, frame_owner,
):
    query_local = queries[0]
    step_count, token_count, width_local = query_local.shape
    heads_local = width_local // HEAD_DIM
    attended = attend_all(
        query_local.reshape(step_count, token_count, heads_local, HEAD_DIM),
        lax.all_gather(key_vecs[0], "seq", axis=1, tiled=True),
        lax.all_gather(value_vecs[0], "seq", axis=1, tiled=True),
    )
    row_count = step_count * token_count
    both_rows = jnp.dot(
        lax.all_gather(attended.reshape(row_count, width_local), "guide", axis=0, tiled=True),
        w_out,
        preferred_element_type=F32,
    )
    half_width = w_out.shape[1]
    swapped = lax.all_to_all(
        both_rows.reshape(2, row_count, half_width), "guide", split_axis=0, concat_axis=2, tiled=True
    )
    projected = swapped.reshape(row_count, 2 * half_width)
    attn_out = lax.psum_scatter(projected, "shard", scatter_dimension=1, tiled=True)
    width_shard = attn_out.shape[1]
    width_model = width_shard * lax.axis_size("shard")
    hidden = residual[0].astype(F32) + attn_gate[:, None, :] * attn_out.reshape(
        step_count, token_count, width_shard
    )
    sum_first, sum_second = lax.psum((jnp.sum(hidden, axis=-1), jnp.sum(hidden * hidden, axis=-1)), "shard")
    mean_row = sum_first / width_model
    var_row = sum_second / width_model - mean_row * mean_row
    inv_std = lax.rsqrt(var_row + norm_epsilon)
    modulated = (hidden - mean_row[..., None]) * inv_std[..., None] * (
        1.0 + norm_scale[:, None, :]
    ) + norm_shift[:, None, :]
    partial_head = jnp.einsum(
        "tqd,dc->tqc", modulated, w_head.astype(F32), precision=lax.Precision.HIGHEST
    )
    predicted = lax.psum(partial_head, "shard")
    seq_count = lax.axis_size("seq")
    frame_group = token_count // seq_count
    frames_view = predicted.reshape(step_count, seq_count, frame_group, predicted.shape[-1])
    owner_table = (
        frame_owner[:, :, None] == jnp.arange(seq_count, dtype=jnp.int32)[None, None, :]
    ).astype(F32)
    by_owner = jnp.einsum("tfo,tfgc->togc", owner_table, frames_view, precision=lax.Precision.HIGHEST)
    arrived = lax.all_to_all(
        lax.all_to_all(by_owner[None], "seq", split_axis=2, concat_axis=3, tiled=True),
        "guide",
        split_axis=4,
        concat_axis=0,
        tiled=True,
    )
    guided = arrived[1] + guidance_scale * (arrived[0] - arrived[1])
    return plan_weight(timesteps)[:, None, None, None] * (guided - noise)


def pack_kernel(parts, half, q_ref, k_ref, v_ref, *out_refs):
    z = lax.axis_index("seq")
    for j in range(parts):
        start = pl.multiple_of(lax.rem(z + j, parts) * half, LANES)
        out_refs[j][0] = k_ref[:, pl.ds(start, half)]
        out_refs[j][1] = v_ref[:, pl.ds(start, half)]
        out_refs[parts + j][...] = q_ref[:, pl.ds(start, half)]


def attend_kernel(parts, *refs):
    q_refs = refs[:parts]
    kv_refs = refs[parts : 3 * parts]
    o_refs = refs[3 * parts :]
    rows = q_refs[0].shape[0]
    for i in range(q_refs[0].shape[1] // HEAD_DIM):
        cols = slice(i * HEAD_DIM, (i + 1) * HEAD_DIM)
        q = jnp.concatenate([r[:, cols] for r in q_refs], axis=0)
        k = jnp.concatenate([r[0, :, cols] for r in kv_refs], axis=0)
        v = jnp.concatenate([r[1, :, cols] for r in kv_refs], axis=0)
        scores = lax.dot_general(q, k, (((1,), (1,)), ((), ())), preferred_element_type=F32)
        scores = scores * (HEAD_DIM ** (-0.5) * LOG2E)
        expo = jnp.exp2(scores - jnp.max(scores, axis=1, keepdims=True))
        total = jnp.sum(expo, axis=1, keepdims=True)
        mixed = jnp.dot(expo.astype(BF16), v, preferred_element_type=F32) / total
        for j in range(parts):
            o_refs[j][:, cols] = mixed[j * rows : (j + 1) * rows].astype(BF16)


def load_weights(parts, half, chunk, take_own, own_ref, other_ref, w_scr, sems):
    z = lax.axis_index("seq")
    copies = []
    for t in range(w_scr.shape[0]):
        for j in range(parts):
            start = pl.multiple_of(lax.rem(z + j, parts) * half, LANES)
            src = (pl.ds(start, half), pl.ds(t * chunk, chunk))
            dst = w_scr.at[t, pl.ds(j * half, half), :]
            copies.append((t, src, dst, sems.at[t, j]))

    @pl.when(take_own)
    def _():
        for _, src, dst, sem in copies:
            pltpu.make_async_copy(own_ref.at[src], dst, sem).start()

    @pl.when(jnp.logical_not(take_own))
    def _():
        for _, src, dst, sem in copies:
            pltpu.make_async_copy(other_ref.at[src], dst, sem).start()

    def wait(t):
        for tt, src, dst, sem in copies:
            if tt == t:
                pltpu.make_async_copy(own_ref.at[src], dst, sem).wait()

    return wait


def project(parts, half, o_refs, w_scr, t):
    total = None
    for j in range(parts):
        term = jnp.dot(o_refs[j][...], w_scr[t, j * half : (j + 1) * half, :], preferred_element_type=F32)
        total = term if total is None else total + term
    return total


def send_kernel(parts, half, chunk, first, count, *refs):
    o_refs = refs[:parts]
    own_ref, other_ref, out_ref, w_scr, sems = refs[parts:]
    take_own = lax.axis_index("guide") != lax.axis_index("shard")
    wait = load_weights(
        parts, half, chunk, take_own,
        own_ref.at[:, pl.ds(first, count)], other_ref.at[:, pl.ds(first, count)], w_scr, sems,
    )
    for t in range(w_scr.shape[0]):
        wait(t)
        out_ref[:, t * chunk : (t + 1) * chunk] = project(parts, half, o_refs, w_scr, t).astype(BF16)


def keep_kernel(parts, half, chunk, *refs):
    o_refs = refs[:parts]
    own_ref, other_ref, res_ref, gate_ref, out_ref, w_scr, sems = refs[parts:]
    take_own = lax.axis_index("guide") == lax.axis_index("shard")
    wait = load_weights(parts, half, chunk, take_own, own_ref, other_ref, w_scr, sems)
    for t in range(w_scr.shape[0]):
        cols = slice(t * chunk, (t + 1) * chunk)
        wait(t)
        out_ref[:, cols] = res_ref[:, cols].astype(F32) + gate_ref[:, cols] * project(
            parts, half, o_refs, w_scr, t
        )


def split_dot(head_t, rows):
    dims = (((1,), (1,)), ((), ()))
    high = rows.astype(BF16)
    low = (rows - high.astype(F32)).astype(BF16)
    return lax.dot_general(head_t, high, dims, preferred_element_type=F32) + lax.dot_general(
        head_t, low, dims, preferred_element_type=F32
    )


def head_rows_kernel(scale_ref, shift_ref, head_ref, out_ref):
    width = scale_ref.shape[1]
    which = lax.broadcasted_iota(jnp.int32, (LANES, width), 0)
    rows = jnp.where(which == 0, 1.0 + scale_ref[...], shift_ref[...])
    high = rows.astype(BF16)
    rest = rows - high.astype(F32)
    mid = rest.astype(BF16)
    low = (rest - mid.astype(F32)).astype(BF16)
    dims = (((1,), (1,)), ((), ()))
    total = None
    for part in (high, mid, low):
        term = lax.dot_general(head_ref[...], part, dims, preferred_element_type=F32)
        total = term if total is None else total + term
    out_ref[...] = total


def head_kernel(first, last, chunk, *refs):
    hid_ref, got_ref, gate_ref, scale_ref, head_ref = refs[:5]
    if first:
        out_refs = refs[5:]
    else:
        prev_refs, out_refs = refs[5:8], refs[8:]
    channels = head_ref.shape[0]
    rows = hid_ref.shape[0]
    acc_one = jnp.zeros((rows, LANES), F32) if first else prev_refs[1][...]
    acc_two = jnp.zeros((rows, LANES), F32) if first else prev_refs[2][...]
    acc_head = jnp.zeros((channels, rows), F32) if first else prev_refs[0][...]
    for t in range(hid_ref.shape[1] // chunk):
        cols = slice(t * chunk, (t + 1) * chunk)
        hidden = hid_ref[:, cols] + gate_ref[:, cols] * got_ref[:, cols].astype(F32)
        for s in range(chunk // LANES):
            piece = hidden[:, s * LANES : (s + 1) * LANES]
            acc_one = acc_one + piece
            acc_two = acc_two + piece * piece
        acc_head = acc_head + split_dot(head_ref[:, cols], hidden * (1.0 + scale_ref[:, cols]))
    if last:
        out_ref = out_refs[0]
        out_ref[0:channels, :] = acc_head
        sum_one = jnp.sum(acc_one.T, axis=0, keepdims=True)
        sum_two = jnp.sum(acc_two.T, axis=0, keepdims=True)
        row = lax.broadcasted_iota(jnp.int32, (SUBLANES, rows), 0)
        out_ref[channels : channels + SUBLANES, :] = jnp.where(row == 0, sum_one, sum_two)
    else:
        out_refs[0][...] = acc_head
        out_refs[1][...] = acc_one
        out_refs[2][...] = acc_two


def norm_kernel(width_model, own_ref, got_ref, rows_own_ref, rows_got_ref, keep_ref, send_ref, eps_scr):
    channels = rows_own_ref.shape[0]
    half_channels = channels // 2
    guide = lax.axis_index("guide")
    head = own_ref[0:channels, :] + got_ref[0:channels, :]
    stats = own_ref[channels : channels + SUBLANES, :] + got_ref[channels : channels + SUBLANES, :]
    mean = stats[0:1] / width_model
    var = stats[1:2] / width_model - mean * mean
    inv_std = lax.rsqrt(var + norm_epsilon)
    scaled = rows_own_ref[:, 0:1] + rows_got_ref[:, 0:1]
    shifted = rows_own_ref[:, 1:2] + rows_got_ref[:, 1:2]
    eps_scr[...] = (head - mean * scaled) * inv_std + shifted
    keep_ref[...] = eps_scr[pl.ds(pl.multiple_of(guide * half_channels, SUBLANES), half_channels), :]
    send_ref[...] = eps_scr[pl.ds(pl.multiple_of((1 - guide) * half_channels, SUBLANES), half_channels), :]


def frame_kernel(seq_count, group, owner_ref, keep_ref, got_ref, *out_refs):
    z = lax.axis_index("seq")
    first = lax.axis_index("guide") == 0
    mine, other = keep_ref[...], got_ref[...]
    eps_cond = jnp.where(first, mine, other)
    eps_free = jnp.where(first, other, mine)
    guided = eps_free + guidance_scale * (eps_cond - eps_free)
    fold = LANES // group
    rows = guided.shape[0] // fold
    lane = lax.broadcasted_iota(jnp.int32, (rows, LANES), 1) // group
    for k in range(seq_count):
        target = lax.rem(z + k, seq_count)
        frame = jnp.int32(0)
        for f in range(seq_count):
            frame = jnp.where(owner_ref[0, f] == target, f, frame)
        packed = jnp.zeros((rows, LANES), F32)
        for j in range(fold):
            shift = lax.rem((j - frame) * group + LANES, LANES)
            rolled = pltpu.roll(guided[j * rows : (j + 1) * rows], shift, axis=1)
            packed = jnp.where(lane == j, rolled, packed)
        out_refs[k][...] = packed


def final_kernel(seq_count, group, steps_ref, noise_ref, *refs):
    piece_refs, out_ref = refs[:seq_count], refs[seq_count]
    z = lax.axis_index("seq")
    fold = LANES // group
    rows = piece_refs[0].shape[0]
    lane = lax.broadcasted_iota(jnp.int32, (rows, LANES), 1) // group
    blocks = []
    for j in range(fold):
        block = jnp.zeros((rows, LANES), F32)
        for k in range(seq_count):
            source = lax.rem(z - k + seq_count, seq_count)
            shift = lax.rem((source - j) * group + LANES, LANES)
            block = jnp.where(lane == source, pltpu.roll(piece_refs[k][...], shift, axis=1), block)
        blocks.append(block)
    pad = jnp.zeros((LANES - rows * fold, LANES), F32)
    framed = jnp.concatenate(blocks + [pad], axis=0).T[:, 0 : rows * fold]
    step = jnp.full((1, 1), steps_ref[0], jnp.int32)
    out_ref[...] = plan_weight(step) * (framed - noise_ref[...])


def call(kernel, outs, args, specs=None, scratch=(), flops=0, moved=0):
    shapes = [jax.ShapeDtypeStruct(s, d) for s, d in outs]
    return pl.pallas_call(
        kernel,
        out_shape=shapes,
        in_specs=specs or [VMEM_SPEC] * len(args),
        out_specs=[VMEM_SPEC] * len(outs),
        scratch_shapes=list(scratch),
        cost_estimate=pl.CostEstimate(flops=flops, bytes_accessed=moved, transcendentals=0),
    )(*args)


def fast_plan(
    queries, key_vecs, value_vecs, residual, w_out, attn_gate, norm_shift, norm_scale, w_head, noise,
    timesteps, frame_owner,
):
    seq_count = lax.axis_size("seq")
    parts = seq_count // 2
    rows, width_local = queries.shape[2:]
    half = width_local // parts
    width_shard = residual.shape[3]
    channels = w_head.shape[1]
    group = rows // seq_count
    width_model = float(width_shard * lax.axis_size("shard"))
    both = [(0, 1), (1, 0)]

    other_w = lax.ppermute(w_out, "guide", both)

    packed = call(
        functools.partial(pack_kernel, parts, half),
        [((2, rows, half), BF16)] * parts + [((rows, half), BF16)] * parts,
        [queries[0, 0], key_vecs[0, 0], value_vecs[0, 0]],
        moved=12 * rows * width_local,
    )
    there = [
        [
            (z * 2 + c, (parts * c + (z + j) % parts) * 2 + z // parts)
            for z in range(seq_count)
            for c in range(2)
        ]
        for j in range(parts)
    ]
    back = [[(b, a) for a, b in pairs] for pairs in there]
    axes = ("seq", "guide")
    kv_own = [lax.ppermute(packed[j], axes, there[j]) for j in range(parts)]
    q_own = [lax.ppermute(packed[parts + j], axes, there[j]) for j in range(parts)]
    kv_other = [lax.ppermute(block, "guide", both) for block in kv_own]

    head_t = w_head.T
    rows_own = call(
        head_rows_kernel, [((channels, LANES), F32)], [norm_scale, norm_shift, head_t],
        moved=4 * width_shard * LANES,
    )[0]
    rows_got = lax.ppermute(rows_own, "shard", both)

    mixed = call(
        functools.partial(attend_kernel, parts),
        [((rows, half), BF16)] * parts,
        q_own + kv_own + kv_other,
        flops=8 * rows * parts * rows * parts * half,
        moved=2 * rows * half * parts * 6,
    )
    mixed = [lax.ppermute(mixed[j], axes, back[j]) for j in range(parts)]

    chunk = 256
    pieces = 2
    width_piece = width_shard // pieces
    tiles = width_piece // chunk
    got = []
    for i in range(pieces):
        partial = call(
            functools.partial(send_kernel, parts, half, chunk, i * width_piece, width_piece),
            [((rows, width_piece), BF16)],
            mixed + [w_out, other_w],
            [VMEM_SPEC] * parts + [ANY_SPEC] * 2,
            [
                pltpu.VMEM((tiles, width_local, chunk), BF16),
                pltpu.SemaphoreType.DMA((tiles, parts)),
            ],
            flops=2 * rows * width_local * width_piece,
            moved=2 * width_local * width_piece,
        )[0]
        got.append(lax.ppermute(partial, "shard", both))
    hidden = call(
        functools.partial(keep_kernel, parts, half, chunk),
        [((rows, width_shard), F32)],
        mixed + [w_out, other_w, residual[0, 0], attn_gate],
        [VMEM_SPEC] * parts + [ANY_SPEC] * 2 + [VMEM_SPEC] * 2,
        [
            pltpu.VMEM((tiles * pieces, width_local, chunk), BF16),
            pltpu.SemaphoreType.DMA((tiles * pieces, parts)),
        ],
        flops=2 * rows * width_local * width_shard,
        moved=2 * width_local * width_shard,
    )[0]
    state = []
    for i in range(pieces):
        first, last = i == 0, i == pieces - 1
        cols = slice(i * width_piece, (i + 1) * width_piece)
        state = call(
            functools.partial(head_kernel, first, last, chunk),
            [((channels + SUBLANES, rows), F32)]
            if last
            else [((channels, rows), F32), ((rows, LANES), F32), ((rows, LANES), F32)],
            [hidden[:, cols], got[i], attn_gate[:, cols], norm_scale[:, cols], head_t[:, cols]] + list(state),
            flops=4 * rows * channels * width_piece,
            moved=6 * rows * width_piece,
        )
    sums = state[0]
    sums_got = lax.ppermute(sums, "shard", both)
    keep, send = call(
        functools.partial(norm_kernel, width_model),
        [((channels // 2, rows), F32)] * 2,
        [sums, sums_got, rows_own, rows_got],
        scratch=[pltpu.VMEM((channels, rows), F32)],
    )
    eps_got = lax.ppermute(send, "guide", both)
    fold = LANES // group
    frames = call(
        functools.partial(frame_kernel, seq_count, group),
        [((channels // 2 // fold, LANES), F32)] * seq_count,
        [frame_owner, keep, eps_got],
        [SMEM_SPEC, VMEM_SPEC, VMEM_SPEC],
    )
    arrived = [frames[0]] + [
        lax.ppermute(frames[k], "seq", [(z, (z + k) % seq_count) for z in range(seq_count)])
        for k in range(1, seq_count)
    ]
    out = call(
        functools.partial(final_kernel, seq_count, group),
        [((rows, channels // 2), F32)],
        [timesteps, noise[0, 0]] + arrived,
        [SMEM_SPEC] + [VMEM_SPEC] * (seq_count + 1),
    )[0]
    return out[None, None]


def fast_fits(sizes, queries, residual, w_out, w_head):
    seq_count = sizes["seq"]
    step_count, rows, width_local = queries.shape[1:]
    channels = w_head.shape[1]
    if sizes["guide"] != 2 or sizes["shard"] != 2 or seq_count % 2 or step_count != 1 or rows != LANES:
        return False
    if width_local % (seq_count // 2 * HEAD_DIM) or residual.shape[3] % (4 * LANES):
        return False
    if w_out.shape[1] != residual.shape[3] or channels % (2 * SUBLANES):
        return False
    group = rows // seq_count
    if rows % seq_count or LANES % group:
        return False
    fold = LANES // group
    return channels // 2 % (fold * SUBLANES) == 0


def solution(mesh):
    sizes = dict(mesh.shape)

    def on_device(queries, key_vecs, value_vecs, residual, w_out, attn_gate, norm_shift, norm_scale, w_head, *rest):
        fits = fast_fits(sizes, queries, residual, w_out, w_head)
        plan = fast_plan if fits else general_plan
        return plan(
            queries, key_vecs, value_vecs, residual, w_out, attn_gate, norm_shift, norm_scale, w_head, *rest
        )

    return jax.shard_map(
        on_device,
        mesh=mesh,
        in_specs=(
            P("guide", "group", "seq", "shard"),
            P("guide", "group", "seq", "shard"),
            P("guide", "group", "seq", "shard"),
            P("guide", "group", "seq", "shard"),
            P("shard", "guide"),
            P("group", "shard"),
            P("group", "shard"),
            P("group", "shard"),
            P("shard", None),
            P("group", "seq", None, "guide"),
            P("group"),
            P("group", None),
        ),
        out_specs=P("group", "seq", None, "guide"),
        check_vma=False,
    )
```

time: 176 us -> 102 us (0.58)
  waiting for transfers between devices: 107 us -> 8.2 us
  starting transfers between devices: 5.09 us -> 43.2 us
  Pallas kernels: 0 us -> 34 us
  blocking collectives: 24.6 us -> 0 us
  between operations: 14 us -> 0.76 us
  matrix products: 10.1 us -> 0 us
  local copies, waits for them, and re-layouts: 10.7 us -> 15 us
  other arithmetic: 3.65 us -> 0 us
    all_gather x2 -> x0, waiting for transfers between devices: 65.6 us -> none  [the longest x1 35.6 us: on_device(): lax.all_gather(key_vecs[0], 'seq', axis=1, tiled=True)]
    ppermute x0 -> x17, starting transfers between devices: none -> 43.2 us  [the longest x2 17.6 us: fast_plan(): kv_other = [lax.ppermute(block, 'guide', both) for block in kv_own]]
    reduce_scatter x1 -> x0, waiting for transfers between devices: 36.1 us -> none  [on_device(): lax.psum_scatter(projected, 'shard', scatter_dimension=1, tiled=True)]
    pallas_call x0 -> x11, Pallas kernels: none -> 34 us  [call(): pl.pallas_call(kernel, out_shape=shapes, in_specs=specs or [VMEM_SPEC] *...]
    psum x2 -> x0, blocking collectives: 12.7 us -> none  [the longest x1 7.79 us: on_device(): predicted = lax.psum(partial_head, 'shard')]
    dot_general x5 -> x0, matrix products: 10.1 us -> none  [the longest x1 4.74 us: on_device(): jnp.dot(lax.all_gather(attended, 'guide', axis=0, tiled=True), w_out, pre...]
    all_to_all x2 -> x0, blocking collectives: 9.6 us -> none  [the longest x1 5.84 us: on_device(): lax.all_to_all(both_rows.reshape(2, row_count, half_width), 'guide', spli...]
    ppermute x0 -> x17, waiting for transfers between devices: none -> 8.2 us  [the longest x1 3.9 us: fast_plan(): rows_got = lax.ppermute(rows_own, 'shard', both)]
  transfers between devices with their start and end apart: 4 -> 17, of which waited for: 4 -> 6; matrix products, arithmetic and copies ran while one was open for 2% -> 8% of each run, Pallas kernels for 0% -> 22%
where the time goes in v1:
time: 102 us; the launch traced here: 101 us
  starting transfers between devices  43.2 us (42%)
  Pallas kernels  34 us (33%)
  local copies, waits for them, and re-layouts  15 us (15%)
  waiting for transfers between devices  8.2 us (8%)
    pallas_call x11, Pallas kernels, call(): pl.pallas_call(kernel, out_shape=shapes, in_specs=specs or [VMEM_SPEC] *...  34 us
    ppermute x2, starting transfers between devices, fast_plan(): kv_other = [lax.ppermute(block, 'guide', both) for block in kv_own]  17.6 us
    unnamed x35, local copies, waits for them, and re-layouts  6.64 us
    ppermute x3, starting transfers between devices, fast_plan(): lax.ppermute(frames[k], 'seq', [(z, (z + k) % seq_count) for z in range(s...  6.51 us
    ppermute x2, starting transfers between devices, fast_plan(): mixed = [lax.ppermute(mixed[j], axes, back[j]) for j in range(parts)]  5.5 us
    ppermute x2, starting transfers between devices, fast_plan(): lax.ppermute(packed[parts + j], axes, there[j])  4.12 us
    ppermute x1, waiting for transfers between devices, fast_plan(): rows_got = lax.ppermute(rows_own, 'shard', both)  3.9 us
    ppermute x1, starting transfers between devices, fast_plan(): eps_got = lax.ppermute(send, 'guide', both)  3.25 us
  transfers between devices with their start and end apart: 17, of which 6 were waited for; matrix products, arithmetic and copies ran while one was open for 8% of the time, Pallas kernels for 22%

profile of v1, /device:TPU:0, one launch (start us, length us, event | category | flops | bytes accessed | tf_op | source)
XLA Modules:
  0.0 101.2 jit_solution(4542334853851167656)
XLA Ops:
  0.5 2.2 %shard_map.118 = (bf16[2,128,640]{2,1,0:T(8,128)(2,1)}, bf16[2,128,640]{2,1,0:T(8,128)(2,1)}, bf16[128,640]{1,0:T(8,128)(2,1)}, bf16[128,640]{1,0:T(8,128)(2,1)}) custom-call(bf16[128,1280]{1,0:T(8,128)(2,1)} %bitcast.10, bf16[128,1280]{1,0:T(8,128)(2,1)} %bitcast.11, bf16[128,1280]{1,0:T(8,128)(2,1)} %bitcast.12), custom_call_target="tpu_custom_call" | custom-call | bytes 1966080 | tf_op jit(solution)/shard_map/pallas_call | solution.py:313
  2.7 1.6 %collective-permute-start = (bf16[128,640]{1,0:T(8,128)(2,1)}, bf16[128,640]{1,0:T(8,128)(2,1)S(1)}, u32[]{:S(2)}, u32[]{:S(2)}) collective-permute-start(bf16[128,640]{1,0:T(8,128)(2,1)} %get-tuple-element.20), channel_id=1, source_target_pairs={{0,0},{1,8},{4,4},{5,12},{8,1},{9,9},{12,5},{13,13},{2,2},{3,10},{... | collective-permute-start | bytes 491528 | tf_op jit(solution)/shard_map/ppermute | solution.py:356
  4.3 2.6 %collective-permute-start.1 = (bf16[128,640]{1,0:T(8,128)(2,1)}, bf16[128,640]{1,0:T(8,128)(2,1)S(1)}, u32[]{:S(2)}, u32[]{:S(2)}) collective-permute-start(bf16[128,640]{1,0:T(8,128)(2,1)} %get-tuple-element.21), channel_id=1, source_target_pairs={{0,4},{1,12},{4,0},{5,8},{8,5},{9,13},{12,1},{13,9},{2,6},{3,14},{... | collective-permute-start | bytes 491528 | tf_op jit(solution)/shard_map/ppermute | solution.py:356
  6.8 1.6 %collective-permute-start.2 = (bf16[2,128,640]{2,1,0:T(8,128)(2,1)}, bf16[2,128,640]{2,1,0:T(8,128)(2,1)S(1)}, u32[]{:S(2)}, u32[]{:S(2)}) collective-permute-start(bf16[2,128,640]{2,1,0:T(8,128)(2,1)} %get-tuple-element.22), channel_id=1, source_target_pairs={{0,0},{1,8},{4,4},{5,12},{8,1},{9,9},{12,5},{13,13},{2,2},{3,10},{... | collective-permute-start | bytes 983048 | tf_op jit(solution)/shard_map/ppermute | solution.py:355
  8.5 1.8 %fusion.1 = (bf16[64,1280]{1,0:T(8,128)(2,1)}, bf16[64,1280]{1,0:T(8,128)(2,1)}) fusion(bf16[64,2560]{1,0:T(8,128)(2,1)} %bitcast.7), kind=kLoop, calls=%fused_computation.1 | loop fusion | bytes 655360 | tf_op jit(solution)/shard_map/slice | solution.py:415
  10.2 17.5 %collective-permute-start.4 = (bf16[2,128,640]{2,1,0:T(8,128)(2,1)S(1)}, bf16[2,128,640]{2,1,0:T(8,128)(2,1)S(1)}, u32[]{:S(2)}, u32[]{:S(2)}) collective-permute-start(bf16[2,128,640]{2,1,0:T(8,128)(2,1)S(1)} %collective-permute-done.2.refs_2_), channel_id=1, source_target_pairs={{0,1},{1,0},{2,3},{3,2},{4,5},{5,4},{6,7},{7,6},{8,9},{9,8},{10,11... | collective-permute-start | bytes 983048 | tf_op jit(solution)/shard_map/ppermute | solution.py:357
  30.8 3.8 %shard_map.119 = (bf16[128,640]{1,0:T(8,128)(2,1)}, bf16[128,640]{1,0:T(8,128)(2,1)}) custom-call(bf16[128,640]{1,0:T(8,128)(2,1)} %copy-done.8, bf16[128,640]{1,0:T(8,128)(2,1)} %copy-done.9, bf16[2,128,640]{2,1,0:T(8,128)(2,1)} %copy-done.2, bf16[2,128,640]{2,1,0:T(8,128)(2,1)} %copy-done.3, bf16[2,128,640]{2,1,0:T(8,128)(2,1)} %copy-done.5, ...), custom_call_target="tpu_custom_call" | custom-call | flops 335544320 | bytes 1966080 | tf_op jit(solution)/shard_map/pallas_call | solution.py:313
  34.6 1.6 %collective-permute-start.6 = (bf16[128,640]{1,0:T(8,128)(2,1)}, bf16[128,640]{1,0:T(8,128)(2,1)S(1)}, u32[]{:S(2)}, u32[]{:S(2)}) collective-permute-start(bf16[128,640]{1,0:T(8,128)(2,1)} %get-tuple-element.24), channel_id=1, source_target_pairs={{0,0},{8,1},{4,4},{12,5},{1,8},{9,9},{5,12},{13,13},{2,2},{10,3},{... | collective-permute-start | bytes 491528 | tf_op jit(solution)/shard_map/ppermute | solution.py:373
  36.2 3.9 %collective-permute-start.7 = (bf16[128,640]{1,0:T(8,128)(2,1)}, bf16[128,640]{1,0:T(8,128)(2,1)S(1)}, u32[]{:S(2)}, u32[]{:S(2)}) collective-permute-start(bf16[128,640]{1,0:T(8,128)(2,1)} %get-tuple-element.25), channel_id=1, source_target_pairs={{4,0},{12,1},{0,4},{8,5},{5,8},{13,9},{1,12},{9,13},{6,2},{14,3},{... | collective-permute-start | bytes 491528 | tf_op jit(solution)/shard_map/ppermute | solution.py:373
  41.4 2.2 %collective-permute-done.7.refs_1_ = bf16[128,640]{1,0:T(8,128)(2,1)S(1)} collective-permute-done((bf16[128,640]{1,0:T(8,128)(2,1)}, bf16[128,640]{1,0:T(8,128)(2,1)S(1)}, u32[]{:S(2)}, u32[]{:S(2)}) %collective-permute-start.7) | collective-permute-done | bytes 163872 | tf_op jit(solution)/shard_map/ppermute | solution.py:373
  44.3 4.6 %shard_map.121 = bf16[128,1280]{1,0:T(8,128)(2,1)} custom-call(bf16[128,640]{1,0:T(8,128)(2,1)} %copy-done, bf16[128,640]{1,0:T(8,128)(2,1)} %copy-done.1, bf16[1280,2560]{1,0:T(8,128)(2,1)} %refs_2_.5, bf16[1280,2560]{1,0:T(8,128)(2,1)} %collective-permute-done.8.refs_3_), custom_call_target="tpu_custom_call" | custom-call | flops 419430400 | bytes 3276800 | tf_op jit(solution)/shard_map/pallas_call | solution.py:313
  49.0 1.7 %collective-permute-start.9 = (bf16[128,1280]{1,0:T(8,128)(2,1)}, bf16[128,1280]{1,0:T(8,128)(2,1)S(1)}, u32[]{:S(2)}, u32[]{:S(2)}) collective-permute-start(bf16[128,1280]{1,0:T(8,128)(2,1)} %shard_map.121), channel_id=1, source_target_pairs={{0,2},{2,0},{1,3},{3,1},{4,6},{6,4},{5,7},{7,5},{8,10},{10,8},{9,1... | collective-permute-start | bytes 983048 | tf_op jit(solution)/shard_map/ppermute | solution.py:393
  50.7 4.6 %shard_map.122 = bf16[128,1280]{1,0:T(8,128)(2,1)} custom-call(bf16[128,640]{1,0:T(8,128)(2,1)} %copy-done, bf16[128,640]{1,0:T(8,128)(2,1)} %copy-done.1, bf16[1280,2560]{1,0:T(8,128)(2,1)} %refs_2_.5, bf16[1280,2560]{1,0:T(8,128)(2,1)} %collective-permute-done.8.refs_3_), custom_call_target="tpu_custom_call" | custom-call | flops 419430400 | bytes 3276800 | tf_op jit(solution)/shard_map/pallas_call | solution.py:313
  55.7 7.2 %shard_map.120 = f32[128,2560]{1,0:T(8,128)} custom-call(bf16[128,640]{1,0:T(8,128)(2,1)} %copy-done, bf16[128,640]{1,0:T(8,128)(2,1)} %copy-done.1, bf16[1280,2560]{1,0:T(8,128)(2,1)} %refs_2_.5, bf16[1280,2560]{1,0:T(8,128)(2,1)} %collective-permute-done.8.refs_3_, bf16[128,2560]{1,0:T(8,128)(2,1)} %bitcast.9, f32[1,2560]{1,0:T(1,128)} %refs_5_.1), custom_call_target="tpu_custom_call" | custom-call | flops 838860800 | bytes 6553600 | tf_op jit(solution)/shard_map/pallas_call | solution.py:313
  62.9 2.4 %fusion = (f32[128,1280]{1,0:T(8,128)}, f32[128,1280]{1,0:T(8,128)}) fusion(f32[128,2560]{1,0:T(8,128)} %shard_map.120), kind=kLoop, calls=%fused_computation | loop fusion | bytes 2621440 | tf_op jit(solution)/shard_map/slice | solution.py:415
  66.3 2.3 %shard_map.123 = (f32[64,128]{1,0:T(8,128)}, f32[128,128]{1,0:T(8,128)}, f32[128,128]{1,0:T(8,128)}) custom-call(f32[128,1280]{1,0:T(8,128)} %get-tuple-element.35.refs_0_, bf16[128,1280]{1,0:T(8,128)(2,1)} %copy-done.7, f32[1,1280]{1,0:T(1,128)} %get-tuple-element.41.refs_2_, f32[1,1280]{1,0:T(1,128)} %get-tuple-element.39.refs_3_, ...), custom_call_target="tpu_custom_call" | custom-call | flops 41943040 | bytes 983040 | tf_op jit(solution)/shard_map/pallas_call | solution.py:313
  69.3 2.3 %shard_map.124.own_ref = f32[72,128]{1,0:T(8,128)} custom-call(f32[128,1280]{1,0:T(8,128)} %get-tuple-element.36.refs_0_, bf16[128,1280]{1,0:T(8,128)(2,1)} %copy-done.4, f32[1,1280]{1,0:T(1,128)} %get-tuple-element.42.refs_2_, f32[1,1280]{1,0:T(1,128)} %get-tuple-element.40.refs_3_, bf16[64,1280]{1,0:T(8,128)(2,1)} %get-tuple-element.38.refs_4_, ...), custom_call_target="tpu_custom_call" | custom-call | flops 41943040 | bytes 983040 | tf_op jit(solution)/shard_map/pallas_call | solution.py:313
  73.0 2.4 %shard_map.125.rows_own_ref = f32[64,128]{1,0:T(8,128)} custom-call(f32[1,2560]{1,0:T(1,128)} %scale_ref.1, f32[1,2560]{1,0:T(1,128)} %shift_ref.1, bf16[64,2560]{1,0:T(8,128)(2,1)} %bitcast.8), custom_call_target="tpu_custom_call" | custom-call | bytes 1310720 | tf_op jit(solution)/shard_map/pallas_call | solution.py:313
  76.0 3.9 %collective-permute-done.12.rows_got_ref = f32[64,128]{1,0:T(8,128)S(1)} collective-permute-done((f32[64,128]{1,0:T(8,128)}, f32[64,128]{1,0:T(8,128)S(1)}, u32[]{:S(2)}, u32[]{:S(2)}) %collective-permute-start.12) | collective-permute-done | bytes 32800 | tf_op jit(solution)/shard_map/ppermute | solution.py:364
  82.6 3.3 %collective-permute-start.13 = (f32[32,128]{1,0:T(8,128)}, f32[32,128]{1,0:T(8,128)S(1)}, u32[]{:S(2)}, u32[]{:S(2)}) collective-permute-start(f32[32,128]{1,0:T(8,128)} %get-tuple-element.30), channel_id=1, source_target_pairs={{0,1},{1,0},{2,3},{3,2},{4,5},{5,4},{6,7},{7,6},{8,9},{9,8},{10,11... | collective-permute-start | bytes 49160 | tf_op jit(solution)/shard_map/ppermute | solution.py:427
  89.0 1.8 %collective-permute-start.14 = (f32[8,128]{1,0:T(8,128)}, f32[8,128]{1,0:T(8,128)S(1)}, u32[]{:S(2)}, u32[]{:S(2)}) collective-permute-start(f32[8,128]{1,0:T(8,128)} %get-tuple-element.32), channel_id=1, source_target_pairs={{0,4},{4,8},{8,12},{12,0},{1,5},{5,9},{9,13},{13,1},{2,6},{6,10},{... | collective-permute-start | bytes 12296 | tf_op jit(solution)/shard_map/ppermute | solution.py:436
  90.8 2.8 %collective-permute-start.15 = (f32[8,128]{1,0:T(8,128)}, f32[8,128]{1,0:T(8,128)S(1)}, u32[]{:S(2)}, u32[]{:S(2)}) collective-permute-start(f32[8,128]{1,0:T(8,128)} %get-tuple-element.33), channel_id=1, source_target_pairs={{0,8},{4,12},{8,0},{12,4},{1,9},{5,13},{9,1},{13,5},{2,10},{6,14},... | collective-permute-start | bytes 12296 | tf_op jit(solution)/shard_map/ppermute | solution.py:436
  93.6 1.8 %collective-permute-start.16 = (f32[8,128]{1,0:T(8,128)}, f32[8,128]{1,0:T(8,128)S(1)}, u32[]{:S(2)}, u32[]{:S(2)}) collective-permute-start(f32[8,128]{1,0:T(8,128)} %get-tuple-element.34), channel_id=1, source_target_pairs={{0,12},{4,0},{8,4},{12,8},{1,13},{5,1},{9,5},{13,9},{2,14},{6,2},{... | collective-permute-start | bytes 12296 | tf_op jit(solution)/shard_map/ppermute | solution.py:436
  98.0 1.7 %shard_map.128 = f32[128,32]{1,0:T(8,128)} custom-call(s32[1]{0:T(128)S(6)} %copy.15.steps_ref, f32[128,32]{1,0:T(8,128)} %bitcast.13, f32[8,128]{1,0:T(8,128)} %get-tuple-element.31.refs_0_, f32[8,128]{1,0:T(8,128)} %copy-done.14, f32[8,128]{1,0:T(8,128)} %copy-done.15, f32[8,128]{1,0:T(8,128)} %copy-done.16), custom_call_target="tpu_custom_call" | custom-call | tf_op jit(solution)/shard_map/pallas_call | solution.py:313
  (61 shorter events, 18.9 us)
Async XLA Ops:
  0.0 43.7 %collective-permute-start.8 = (bf16[1280,2560]{1,0:T(8,128)(2,1)}, bf16[1280,2560]{1,0:T(8,128)(2,1)}, u32[]{:S(2)}, u32[]{:S(2)}) collective-permute-start(bf16[1280,2560]{1,0:T(8,128)(2,1)} %refs_2_.5), channel_id=1, source_target_pairs={{0,1},{1,0},{2,3},{3,2},{4,5},{5,4},{6,7},{7,6},{8,9},{9,8},{10,11... | collective-permute-start | bytes 19660808 | tf_op jit(solution)/shard_map/ppermute | solution.py:337
  2.7 26.5 %collective-permute-start = (bf16[128,640]{1,0:T(8,128)(2,1)}, bf16[128,640]{1,0:T(8,128)(2,1)S(1)}, u32[]{:S(2)}, u32[]{:S(2)}) collective-permute-start(bf16[128,640]{1,0:T(8,128)(2,1)} %get-tuple-element.20), channel_id=1, source_target_pairs={{0,0},{1,8},{4,4},{5,12},{8,1},{9,9},{12,5},{13,13},{2,2},{3,10},{... | collective-permute-start | bytes 491528 | tf_op jit(solution)/shard_map/ppermute | solution.py:356
  4.3 24.9 %collective-permute-start.1 = (bf16[128,640]{1,0:T(8,128)(2,1)}, bf16[128,640]{1,0:T(8,128)(2,1)S(1)}, u32[]{:S(2)}, u32[]{:S(2)}) collective-permute-start(bf16[128,640]{1,0:T(8,128)(2,1)} %get-tuple-element.21), channel_id=1, source_target_pairs={{0,4},{1,12},{4,0},{5,8},{8,5},{9,13},{12,1},{13,9},{2,6},{3,14},{... | collective-permute-start | bytes 491528 | tf_op jit(solution)/shard_map/ppermute | solution.py:356
  6.8 3.4 %collective-permute-start.2 = (bf16[2,128,640]{2,1,0:T(8,128)(2,1)}, bf16[2,128,640]{2,1,0:T(8,128)(2,1)S(1)}, u32[]{:S(2)}, u32[]{:S(2)}) collective-permute-start(bf16[2,128,640]{2,1,0:T(8,128)(2,1)} %get-tuple-element.22), channel_id=1, source_target_pairs={{0,0},{1,8},{4,4},{5,12},{8,1},{9,9},{12,5},{13,13},{2,2},{3,10},{... | collective-permute-start | bytes 983048 | tf_op jit(solution)/shard_map/ppermute | solution.py:355
  8.4 19.3 %collective-permute-start.3 = (bf16[2,128,640]{2,1,0:T(8,128)(2,1)}, bf16[2,128,640]{2,1,0:T(8,128)(2,1)S(1)}, u32[]{:S(2)}, u32[]{:S(2)}) collective-permute-start(bf16[2,128,640]{2,1,0:T(8,128)(2,1)} %get-tuple-element.23), channel_id=1, source_target_pairs={{0,4},{1,12},{4,0},{5,8},{8,5},{9,13},{12,1},{13,9},{2,6},{3,14},{... | collective-permute-start | bytes 983048 | tf_op jit(solution)/shard_map/ppermute | solution.py:355
  10.2 19.2 %copy-start.2 = (bf16[2,128,640]{2,1,0:T(8,128)(2,1)}, bf16[2,128,640]{2,1,0:T(8,128)(2,1)S(1)}, u32[]{:S(2)}) copy-start(bf16[2,128,640]{2,1,0:T(8,128)(2,1)S(1)} %collective-permute-done.2.refs_2_) | copy-start | bytes 983044
  10.2 19.0 %collective-permute-start.4 = (bf16[2,128,640]{2,1,0:T(8,128)(2,1)S(1)}, bf16[2,128,640]{2,1,0:T(8,128)(2,1)S(1)}, u32[]{:S(2)}, u32[]{:S(2)}) collective-permute-start(bf16[2,128,640]{2,1,0:T(8,128)(2,1)S(1)} %collective-permute-done.2.refs_2_), channel_id=1, source_target_pairs={{0,1},{1,0},{2,3},{3,2},{4,5},{5,4},{6,7},{7,6},{8,9},{9,8},{10,11... | collective-permute-start | bytes 983048 | tf_op jit(solution)/shard_map/ppermute | solution.py:357
  27.7 1.7 %copy-start.3 = (bf16[2,128,640]{2,1,0:T(8,128)(2,1)}, bf16[2,128,640]{2,1,0:T(8,128)(2,1)S(1)}, u32[]{:S(2)}) copy-start(bf16[2,128,640]{2,1,0:T(8,128)(2,1)S(1)} %collective-permute-done.3.refs_3_) | copy-start | bytes 983044
  27.7 1.7 %collective-permute-start.5 = (bf16[2,128,640]{2,1,0:T(8,128)(2,1)S(1)}, bf16[2,128,640]{2,1,0:T(8,128)(2,1)S(1)}, u32[]{:S(2)}, u32[]{:S(2)}) collective-permute-start(bf16[2,128,640]{2,1,0:T(8,128)(2,1)S(1)} %collective-permute-done.3.refs_3_), channel_id=1, source_target_pairs={{0,1},{1,0},{2,3},{3,2},{4,5},{5,4},{6,7},{7,6},{8,9},{9,8},{10,11... | collective-permute-start | bytes 983048 | tf_op jit(solution)/shard_map/ppermute | solution.py:357
  29.2 0.7 copy-start.9
  29.2 0.8 copy-start.5
  30.0 0.8 copy-start.6
  34.6 6.8 %collective-permute-start.6 = (bf16[128,640]{1,0:T(8,128)(2,1)}, bf16[128,640]{1,0:T(8,128)(2,1)S(1)}, u32[]{:S(2)}, u32[]{:S(2)}) collective-permute-start(bf16[128,640]{1,0:T(8,128)(2,1)} %get-tuple-element.24), channel_id=1, source_target_pairs={{0,0},{8,1},{4,4},{12,5},{1,8},{9,9},{5,12},{13,13},{2,2},{10,3},{... | collective-permute-start | bytes 491528 | tf_op jit(solution)/shard_map/ppermute | solution.py:373
  36.2 7.5 %collective-permute-start.7 = (bf16[128,640]{1,0:T(8,128)(2,1)}, bf16[128,640]{1,0:T(8,128)(2,1)S(1)}, u32[]{:S(2)}, u32[]{:S(2)}) collective-permute-start(bf16[128,640]{1,0:T(8,128)(2,1)} %get-tuple-element.25), channel_id=1, source_target_pairs={{4,0},{12,1},{0,4},{8,5},{5,8},{13,9},{1,12},{9,13},{6,2},{14,3},{... | collective-permute-start | bytes 491528 | tf_op jit(solution)/shard_map/ppermute | solution.py:373
  41.4 2.2 %copy-start = (bf16[128,640]{1,0:T(8,128)(2,1)}, bf16[128,640]{1,0:T(8,128)(2,1)S(1)}, u32[]{:S(2)}) copy-start(bf16[128,640]{1,0:T(8,128)(2,1)S(1)} %collective-permute-done.6.refs_0_) | copy-start | bytes 491524
  49.0 19.6 %collective-permute-start.9 = (bf16[128,1280]{1,0:T(8,128)(2,1)}, bf16[128,1280]{1,0:T(8,128)(2,1)S(1)}, u32[]{:S(2)}, u32[]{:S(2)}) collective-permute-start(bf16[128,1280]{1,0:T(8,128)(2,1)} %shard_map.121), channel_id=1, source_target_pairs={{0,2},{2,0},{1,3},{3,1},{4,6},{6,4},{5,7},{7,5},{8,10},{10,8},{9,1... | collective-permute-start | bytes 983048 | tf_op jit(solution)/shard_map/ppermute | solution.py:393
  55.3 10.2 %collective-permute-start.10 = (bf16[128,1280]{1,0:T(8,128)(2,1)}, bf16[128,1280]{1,0:T(8,128)(2,1)S(1)}, u32[]{:S(2)}, u32[]{:S(2)}) collective-permute-start(bf16[128,1280]{1,0:T(8,128)(2,1)} %shard_map.122), channel_id=1, source_target_pairs={{0,2},{2,0},{1,3},{3,1},{4,6},{6,4},{5,7},{7,5},{8,10},{10,8},{9,1... | collective-permute-start | bytes 983048 | tf_op jit(solution)/shard_map/ppermute | solution.py:393
  55.7 40.4 %copy-start.12 = (f32[1,1,128,32]{2,3,1,0:T(8,128)S(1)}, f32[1,1,128,32]{2,3,1,0:T(8,128)}, u32[]{:S(2)}) copy-start(f32[1,1,128,32]{2,3,1,0:T(8,128)} %param.21) | copy-start | bytes 49156
  71.5 8.3 %collective-permute-start.11 = (f32[72,128]{1,0:T(8,128)}, f32[72,128]{1,0:T(8,128)S(1)}, u32[]{:S(2)}, u32[]{:S(2)}) collective-permute-start(f32[72,128]{1,0:T(8,128)} %shard_map.124.own_ref), channel_id=1, source_target_pairs={{0,2},{2,0},{1,3},{3,1},{4,6},{6,4},{5,7},{7,5},{8,10},{10,8},{9,1... | collective-permute-start | bytes 110600 | tf_op jit(solution)/shard_map/ppermute | solution.py:420
  75.4 4.4 %collective-permute-start.12 = (f32[64,128]{1,0:T(8,128)}, f32[64,128]{1,0:T(8,128)S(1)}, u32[]{:S(2)}, u32[]{:S(2)}) collective-permute-start(f32[64,128]{1,0:T(8,128)} %shard_map.125.rows_own_ref), channel_id=1, source_target_pairs={{0,2},{2,0},{1,3},{3,1},{4,6},{6,4},{5,7},{7,5},{8,10},{10,8},{9,1... | collective-permute-start | bytes 98312 | tf_op jit(solution)/shard_map/ppermute | solution.py:364
  82.6 4.3 %collective-permute-start.13 = (f32[32,128]{1,0:T(8,128)}, f32[32,128]{1,0:T(8,128)S(1)}, u32[]{:S(2)}, u32[]{:S(2)}) collective-permute-start(f32[32,128]{1,0:T(8,128)} %get-tuple-element.30), channel_id=1, source_target_pairs={{0,1},{1,0},{2,3},{3,2},{4,5},{5,4},{6,7},{7,6},{8,9},{9,8},{10,11... | collective-permute-start | bytes 49160 | tf_op jit(solution)/shard_map/ppermute | solution.py:427
  89.0 7.9 %collective-permute-start.14 = (f32[8,128]{1,0:T(8,128)}, f32[8,128]{1,0:T(8,128)S(1)}, u32[]{:S(2)}, u32[]{:S(2)}) collective-permute-start(f32[8,128]{1,0:T(8,128)} %get-tuple-element.32), channel_id=1, source_target_pairs={{0,4},{4,8},{8,12},{12,0},{1,5},{5,9},{9,13},{13,1},{2,6},{6,10},{... | collective-permute-start | bytes 12296 | tf_op jit(solution)/shard_map/ppermute | solution.py:436
  90.8 6.1 %collective-permute-start.15 = (f32[8,128]{1,0:T(8,128)}, f32[8,128]{1,0:T(8,128)S(1)}, u32[]{:S(2)}, u32[]{:S(2)}) collective-permute-start(f32[8,128]{1,0:T(8,128)} %get-tuple-element.33), channel_id=1, source_target_pairs={{0,8},{4,12},{8,0},{12,4},{1,9},{5,13},{9,1},{13,5},{2,10},{6,14},... | collective-permute-start | bytes 12296 | tf_op jit(solution)/shard_map/ppermute | solution.py:436
  93.6 3.8 %collective-permute-start.16 = (f32[8,128]{1,0:T(8,128)}, f32[8,128]{1,0:T(8,128)S(1)}, u32[]{:S(2)}, u32[]{:S(2)}) collective-permute-start(f32[8,128]{1,0:T(8,128)} %get-tuple-element.34), channel_id=1, source_target_pairs={{0,12},{4,0},{8,4},{12,8},{1,13},{5,1},{9,5},{13,9},{2,14},{6,2},{... | collective-permute-start | bytes 12296 | tf_op jit(solution)/shard_map/ppermute | solution.py:436
  (10 other events, 6.4 us)
